TPU v7x, 768 devices: a whole 4x8x12 slice. The times are simulated.
768 devices in a mesh: rows: 256 (over z_lo, y, x, core), rep: 3 (over z_hi).
Axes of the slice: x: 4, y: 8, z: 12 (z_hi: 3, z_lo: 4; z = z_hi * 4 + z_lo), core: 2. Of those that a mesh axis runs over, the one named last changes fastest.
Arguments:
- features: bfloat16 [32768, 256], P('rows'), may hold values from -6 to 6
- weight: bfloat16 [256, 256], replicated, may hold values from -0.375 to 0.375
- beta: float32 [1], replicated, may hold values from 1 to 4
- edge_bits: int32 [256, 16, 32768], P(None, None, 'rows'), may hold values from 0 to 255, as said below
Outputs:
- aggregated: bfloat16 [32768, 256], P('rows')
Inputs may be any that keep to these rules, and one draw needn't show every extreme that they name: Only the low 8 bits of a word are used; bit c of word w of edge_bits[b, w, n] is set for n = b * 128 + 8 * w + c (self edges); the words of a block pair with no other edges hold only these bits or are zero.
All inputs are finite; a program needn't handle non-finite values.
Results may differ from a plain program's by a relative error of at most 0.0051.
Values may be sent and summed in bfloat16 or wider, within the bound.
A program may use at most 128 MiB of HBM per device.

v0:
```python
import jax
import jax.numpy as jnp
from jax import lax
from jax.sharding import PartitionSpec as P


def shifted(shard, axis, by):
    length = lax.axis_size(axis)
    return lax.ppermute(shard, axis, [(i, (i + by) % length) for i in range(length)])


def inverse_norms(values):
    widened = values.astype(jnp.float32)
    return lax.rsqrt(jnp.sum(widened * widened, axis=1) + 1e-06)


def unpack_flags(packed):
    offsets = jnp.arange(8, dtype=jnp.int32)
    edge_flags = jnp.right_shift(packed[:, None, :], offsets[None, :, None]) & 1
    return edge_flags.reshape(packed.shape[0] * 8, packed.shape[1])


def tile_terms(target_rows, target_scale, source_panel, flags, temper):
    source_scale = inverse_norms(source_panel)
    scores = lax.dot_general(
        source_panel, target_rows, (((1,), (1,)), ((), ())), preferred_element_type=jnp.float32
    )
    scores = scores * source_scale[:, None] * target_scale[None, :] * temper
    weights = jnp.where(flags, jnp.exp(scores - temper), 0.0)
    totals = jnp.sum(weights, axis=0)
    weighted = lax.dot_general(
        weights.astype(jnp.bfloat16),
        source_panel,
        (((0,), (0,)), ((), ())),
        preferred_element_type=jnp.float32,
    )
    return (totals, weighted)


def on_device(features, weight, beta, edge_bits):
    block_count = lax.axis_size("rows")
    replicas = lax.axis_size("rep")
    position = lax.axis_index("rows")
    replica = lax.axis_index("rep")
    section_count = (block_count + replicas - 1) // replicas
    temper = beta[0]
    local_rows = jnp.dot(features, weight, preferred_element_type=jnp.float32).astype(jnp.bfloat16)
    local_scale = inverse_norms(local_rows)
    block_size = local_rows.shape[0]

    def add_terms(state, source_panel, flags):
        part_totals, part_weighted = tile_terms(
            local_rows, local_scale, source_panel, flags, temper
        )
        return (state[0] + part_totals, state[1] + part_weighted)

    def accumulate(state, source_panel, section_no):
        source = (position - section_no) % block_count
        packed = lax.dynamic_index_in_dim(edge_bits, source, 0, keepdims=False)
        packed = jnp.where(section_no < block_count, packed, 0)
        return add_terms(state, source_panel, unpack_flags(packed) == 1)

    empty = (jnp.zeros((block_size,), jnp.float32), jnp.zeros(local_rows.shape, jnp.float32))
    moving = local_rows
    first_panel = local_rows
    for offset_no in range(1, replicas):
        moving = shifted(moving, "rows", 1)
        first_panel = jnp.where(replica == offset_no, moving, first_panel)
    state = accumulate(empty, first_panel, replica)

    def strided_step(step_no, carry):
        source_panel, totals, weighted = carry
        source_panel = shifted(source_panel, "rows", replicas)
        totals, weighted = accumulate(
            (totals, weighted), source_panel, replica + step_no * replicas
        )
        return (source_panel, totals, weighted)

    final = lax.fori_loop(1, section_count, strided_step, (first_panel, state[0], state[1]))
    totals, weighted = lax.psum((final[1], final[2]), "rep")
    return (weighted / totals[:, None]).astype(jnp.bfloat16)


def solution(mesh):
    return jax.shard_map(
        on_device,
        mesh=mesh,
        in_specs=(P("rows", None), P(), P(), P(None, None, "rows")),
        out_specs=P("rows", None),
        check_vma=False,
    )
```

profile of v0, /device:TPU:1, one launch (start us, length us, event | category | flops | bytes accessed | tf_op | source)
XLA Modules:
  0.0 1217.6 jit_solution(12171545984078915328)
XLA Ops:
  24.2 9.0 collective-permute-done.2
  33.7 1095.5 %while.19 = (s32[]{:T(128)}, bf16[128,256]{1,0:T(8,128)(2,1)S(1)}, f32[128]{0:T(128)S(1)}, f32[128,256]{1,0:T(8,128)S(1)}, s32[]{:T(128)}, /*index=5*/s32[]{:T(1...) while((s32[]{:T(128)}, bf16[128,256]{1,0:T(8,128)(2,1)S(1)}, ...), condition=%wide.region_6.7_spmd, body=%wide.region_3.6_spmd.sunk | while | flops 17074196 | bytes 1014650 | solution.py:79
  36.5 9.4 collective-permute-done
  49.9 9.3 collective-permute-done
  63.2 9.1 collective-permute-done
  76.3 8.8 collective-permute-done
  89.1 8.8 collective-permute-done
  101.9 8.8 collective-permute-done
  114.7 8.8 collective-permute-done
  127.5 8.8 collective-permute-done
  140.4 8.8 collective-permute-done
  153.2 8.8 collective-permute-done
  166.0 8.8 collective-permute-done
  178.8 8.8 collective-permute-done
  191.6 8.8 collective-permute-done
  204.4 8.8 collective-permute-done
  268.4 8.9 collective-permute-done
  281.3 9.2 collective-permute-done
  294.5 9.5 collective-permute-done
  308.0 9.3 collective-permute-done
  321.2 9.1 collective-permute-done
  385.6 8.8 collective-permute-done
  398.4 8.8 collective-permute-done
  411.2 8.8 collective-permute-done
  424.0 8.8 collective-permute-done
  436.8 8.8 collective-permute-done
  449.6 8.8 collective-permute-done
  462.4 8.8 collective-permute-done
  475.2 8.8 collective-permute-done
  488.0 8.8 collective-permute-done
  500.8 8.8 collective-permute-done
  513.7 8.8 collective-permute-done
  526.5 8.8 collective-permute-done
  539.3 8.8 collective-permute-done
  552.1 8.8 collective-permute-done
  628.9 8.8 collective-permute-done
  641.7 8.8 collective-permute-done
  654.5 8.8 collective-permute-done
  667.4 8.9 collective-permute-done
  680.2 9.2 collective-permute-done
  693.4 9.5 collective-permute-done
  706.8 9.3 collective-permute-done
  720.1 9.1 collective-permute-done
  733.2 8.8 collective-permute-done
  746.0 8.8 collective-permute-done
  758.8 8.8 collective-permute-done
  771.6 8.8 collective-permute-done
  784.4 8.8 collective-permute-done
  861.2 8.8 collective-permute-done
  874.1 8.8 collective-permute-done
  886.9 8.8 collective-permute-done
  899.7 8.8 collective-permute-done
  912.5 8.9 collective-permute-done
  925.3 9.1 collective-permute-done
  938.4 9.4 collective-permute-done
  951.8 9.3 collective-permute-done
  965.2 9.1 collective-permute-done
  978.3 8.8 collective-permute-done
  991.1 8.9 collective-permute-done
  1055.2 8.8 collective-permute-done
  1068.0 8.8 collective-permute-done
  1080.8 8.8 collective-permute-done
  1093.6 8.8 collective-permute-done
  1138.3 70.8 %all-reduce.2.cloned.1.call-done = f32[128,256]{1,0:T(8,128)} async-done(((f32[128,256]{1,0:T(8,128)}), f32[128,256]{1,0:T(8,128)}) %all-reduce.2.cloned.1.call-update) | async-done | bytes 131088 | tf_op jit(solution)/shard_map/psum | solution.py:80
  (893 shorter events, 570.3 us)
Async XLA Ops:
  6.5 1202.6 %all-reduce.2.cloned.1.call-start = ((), (), s32[]{:S(2)}) async-start(), calls=%async_computation | async-start | bytes 262144 | tf_op jit(solution)/shard_map/psum | solution.py:80
  8.4 13.2 %collective-permute-start.1 = (bf16[128,256]{1,0:T(8,128)(2,1)S(1)}, bf16[128,256]{1,0:T(8,128)(2,1)S(1)}, u32[]{:S(2)}, u32[]{:S(2)}) collective-permute-start(bf16[128,256]{1,0:T(8,128)(2,1)S(1)} %convolution_convert_fusion), channel_id=1, source_target_pairs={{0,3},{3,6},{6,9},{9,12},{12,15},{15,18},{18,21},{21,24},{24,27},{... | collective-permute-start | bytes 196616 | tf_op jit(solution)/shard_map/ppermute | solution.py:9
  33.7 12.2 %collective-permute-start = (bf16[128,256]{1,0:T(8,128)(2,1)S(1)}, bf16[128,256]{1,0:T(8,128)(2,1)S(1)}, u32[]{:S(2)}, u32[]{:S(2)}) collective-permute-start(bf16[128,256]{1,0:T(8,128)(2,1)S(1)} %get-tuple-element.365), channel_id=1, source_target_pairs={{0,9},{3,12},{6,15},{9,18},{12,21},{15,24},{18,27},{21,30},{24,33}... | collective-permute-start | bytes 196616 | tf_op jit(solution)/shard_map/while/body/eval_jaxpr/ppermute | solution.py:9
  47.2 12.1 collective-permute-start
  60.5 11.9 collective-permute-start
  73.6 11.6 collective-permute-start
  86.4 11.6 collective-permute-start
  99.2 11.6 collective-permute-start
  112.0 11.6 collective-permute-start
  124.8 11.6 collective-permute-start
  137.6 11.6 collective-permute-start
  150.4 11.6 collective-permute-start
  163.2 11.6 collective-permute-start
  176.0 11.6 collective-permute-start
  188.8 11.6 collective-permute-start
  201.6 11.6 collective-permute-start
  214.4 11.6 collective-permute-start
  227.3 11.6 collective-permute-start
  240.1 11.6 collective-permute-start
  252.9 11.6 collective-permute-start
  265.7 11.7 collective-permute-start
  278.6 12.0 collective-permute-start
  291.7 12.3 %collective-permute-start = (bf16[128,256]{1,0:T(8,128)(2,1)S(1)}, bf16[128,256]{1,0:T(8,128)(2,1)S(1)}, u32[]{:S(2)}, u32[]{:S(2)}) collective-permute-start(bf16[128,256]{1,0:T(8,128)(2,1)S(1)} %get-tuple-element.365), channel_id=1, source_target_pairs={{0,9},{3,12},{6,15},{9,18},{12,21},{15,24},{18,27},{21,30},{24,33}... | collective-permute-start | bytes 196616 | tf_op jit(solution)/shard_map/while/body/eval_jaxpr/ppermute | solution.py:9
  305.2 12.1 collective-permute-start
  318.5 11.9 collective-permute-start
  331.6 11.6 collective-permute-start
  344.4 11.6 collective-permute-start
  357.2 11.6 collective-permute-start
  382.8 11.6 collective-permute-start
  395.6 11.6 collective-permute-start
  408.4 11.6 collective-permute-start
  421.2 11.6 collective-permute-start
  434.0 11.6 collective-permute-start
  446.8 11.6 collective-permute-start
  459.7 11.6 collective-permute-start
  472.5 11.6 collective-permute-start
  485.3 11.6 collective-permute-start
  498.1 11.6 collective-permute-start
  510.9 11.6 collective-permute-start
  523.7 11.6 collective-permute-start
  536.5 11.6 collective-permute-start
  549.3 11.6 collective-permute-start
  562.1 11.6 collective-permute-start
  574.9 11.6 collective-permute-start
  587.7 11.6 collective-permute-start
  600.5 11.6 collective-permute-start
  626.2 11.6 collective-permute-start
  639.0 11.6 collective-permute-start
  651.8 11.6 collective-permute-start
  664.6 11.6 collective-permute-start
  677.4 12.0 collective-permute-start
  690.6 12.3 %collective-permute-start = (bf16[128,256]{1,0:T(8,128)(2,1)S(1)}, bf16[128,256]{1,0:T(8,128)(2,1)S(1)}, u32[]{:S(2)}, u32[]{:S(2)}) collective-permute-start(bf16[128,256]{1,0:T(8,128)(2,1)S(1)} %get-tuple-element.365), channel_id=1, source_target_pairs={{0,9},{3,12},{6,15},{9,18},{12,21},{15,24},{18,27},{21,30},{24,33}... | collective-permute-start | bytes 196616 | tf_op jit(solution)/shard_map/while/body/eval_jaxpr/ppermute | solution.py:9
  704.1 12.1 collective-permute-start
  717.4 11.8 collective-permute-start
  730.4 11.6 collective-permute-start
  743.2 11.6 collective-permute-start
  756.0 11.6 collective-permute-start
  768.8 11.6 collective-permute-start
  909.7 11.6 collective-permute-start
  922.6 11.9 collective-permute-start
  935.7 12.2 %collective-permute-start = (bf16[128,256]{1,0:T(8,128)(2,1)S(1)}, bf16[128,256]{1,0:T(8,128)(2,1)S(1)}, u32[]{:S(2)}, u32[]{:S(2)}) collective-permute-start(bf16[128,256]{1,0:T(8,128)(2,1)S(1)} %get-tuple-element.365), channel_id=1, source_target_pairs={{0,9},{3,12},{6,15},{9,18},{12,21},{15,24},{18,27},{21,30},{24,33}... | collective-permute-start | bytes 196616 | tf_op jit(solution)/shard_map/while/body/eval_jaxpr/ppermute | solution.py:9
  949.1 12.1 collective-permute-start
  962.4 11.9 collective-permute-start
  988.3 11.6 collective-permute-start
  (26 other events, 280.0 us)
Sparse Core Ops, SparseCore 0:
  1130.1 79.0 all-reduce.1
where the time goes:
time: 1230 us; the launch traced here: 1220 us
  waiting for transfers between devices  846 us (69%)
  starting transfers between devices  170 us (14%)
  matrix products  90.3 us (7%)
  other arithmetic  72.4 us (6%)
  between operations  14.1 us (1%)
    ppermute x87, waiting for transfers between devices, shifted(): lax.ppermute(shard, axis, [(i, (i + by) % length) for i in range(length)])  775 us
    ppermute x87, starting transfers between devices, shifted(): lax.ppermute(shard, axis, [(i, (i + by) % length) for i in range(length)])  170 us
    dot_general x86, matrix products, tile_terms(): lax.dot_general(source_panel, target_rows, (((1,), (1,)), ((), ())), pref...  72.3 us
    psum x1, waiting for transfers between devices, on_device(): totals, weighted = lax.psum((final[1], final[2]), 'rep')  70.8 us
    select_n x86, other arithmetic, accumulate(): packed = jnp.where(section_no < block_count, packed, 0)  60.5 us
  transfers between devices with their start and end apart: 88, of which 88 were waited for; matrix products, arithmetic and copies ran while one was open for 6% of the time, Pallas kernels for 0%

commit v1 on v0

v1 whole, which is shorter than its diff:
```python
import functools
import math

import jax
import jax.numpy as jnp
from jax import lax
from jax.experimental import pallas as pl
from jax.experimental.pallas import tpu as pltpu
from jax.sharding import PartitionSpec as P

MESH = pl.DeviceIdType.MESH
NX, NY, NZ, REPS = 4, 8, 4, 3
ROWS, F = 128, 256
PART, STRIDE = 48, 40
COLUMN, UA, UB = 192, 80, 112
A_GROUPS = [divmod(i, 6) for i in range(UA // 8)]
B_GROUPS = [divmod(i, 6) for i in range(UA // 8, COLUMN // 8)]
LOG2E = math.log2(math.e)


def kernel(
    features, weight, beta, edges, out,
    feat_v, weight_v, own_p, sib_p, stage, targets_t, own_e, sib_e,
    column, ax, ay, by, bx, acc, total, part_in, tot_out, tot_in, red, red_tot,
    load_sem, edge_sem, z_send, z_recv, s_send, s_recv,
    ax_send, ax_recv, ay_send, ay_recv, by_send, by_recv, bx_send, bx_recv,
    r_send, r_recv,
):
    me = lax.axis_index("rows")
    rep = lax.axis_index("rep")
    core = lax.rem(me, 2)
    x = lax.rem(lax.div(me, 2), NX)
    y = lax.rem(lax.div(me, 2 * NX), NY)
    zl = lax.div(me, 2 * NX * NY)
    depth = NZ * REPS
    z = rep * NZ + zl

    def device(dx=0, dy=0, dz=0, on=core):
        there = lax.rem(z + dz + depth, depth)
        row = lax.rem(there, NZ)
        row = row * NY + lax.rem(y + dy + NY, NY)
        row = row * NX + lax.rem(x + dx + NX, NX)
        return (row * 2 + on, lax.div(there, NZ))

    sibling = device(on=1 - core)
    x_up, x_down, x_far = device(dx=1), device(dx=-1), device(dx=2)
    y_up, y_down = device(dy=1), device(dy=-1)
    z_up, z_down = device(dz=1), device(dz=-1)
    z_up2, z_down2 = device(dz=2), device(dz=-2)
    z_far = device(dz=2 - 4 * core)
    r_up, r_down = device(dz=NZ), device(dz=-NZ)

    barrier = pltpu.get_barrier_semaphore()
    greeted = (sibling, x_up, x_down, x_far, y_up, y_down, z_up, z_down, z_up2, z_down2, r_up, r_down)
    for other in greeted:
        pl.semaphore_signal(barrier, inc=1, device_id=other, device_id_type=MESH)

    loads = [
        pltpu.make_async_copy(features, feat_v, load_sem.at[0]),
        pltpu.make_async_copy(weight, weight_v, load_sem.at[1]),
    ]
    for load in loads:
        load.start()
    edge_load = pltpu.make_async_copy(edges.at[:, core], own_e, edge_sem)
    edge_load.start()
    for load in loads:
        load.wait()
    rows = jnp.dot(feat_v[...], weight_v[...], preferred_element_type=jnp.float32)
    rows = rows.astype(jnp.bfloat16)
    own_p[...] = rows
    for r in range(REPS):
        stage[r] = rows[r * STRIDE : r * STRIDE + PART]
    pl.semaphore_wait(barrier, len(greeted))

    def remote(src, dst, send, recv, to):
        return pltpu.make_async_remote_copy(
            src_ref=src, dst_ref=dst, send_sem=send, recv_sem=recv, device_id=to, device_id_type=MESH
        )

    own_rows = column.at[pl.ds(pl.multiple_of(zl * PART, 16), PART)]

    def z_copy(slot, to):
        return remote(stage.at[to[1]], own_rows, z_send.at[slot], z_recv.at[slot], to)

    z_copies = [z_copy(0, z_up), z_copy(1, z_down), z_copy(2, z_far)]
    for copy in z_copies:
        copy.start()
    p_copy = remote(own_p, sib_p, s_send.at[0], s_recv.at[0], sibling)
    p_copy.start()
    e_copy = remote(edges.at[:, 1 - core], sib_e, s_send.at[1], s_recv.at[1], sibling)
    e_copy.start()
    own_copy = pltpu.make_async_copy(stage.at[rep], own_rows, load_sem.at[0])
    own_copy.start()

    bits = jnp.left_shift(jnp.int32(1), lax.broadcasted_iota(jnp.int32, (8, ROWS), 0))
    first_bits = jnp.where(rep == 0, bits, 0)
    temper = beta[0]
    shift = temper * LOG2E
    acc[...] = jnp.zeros_like(acc)
    total[...] = jnp.zeros_like(total)
    by[3, 1] = jnp.zeros((UB, F), jnp.bfloat16)

    p_copy.wait_recv()
    both = jnp.concatenate([own_p[...].astype(jnp.float32), sib_p[...].astype(jnp.float32)], axis=0)
    turned = both.T
    targets_t[...] = turned.astype(jnp.bfloat16)
    squares = jnp.sum(turned * turned, axis=0, keepdims=True)
    target_scale = lax.rsqrt(squares + 1e-06) * shift

    def column_groups(groups, dx, dy, live=None):
        there_x = lax.rem(x + dx + NX, NX)
        there_y = lax.rem(y + dy + NY, NY)
        return [(zc, there_y, there_x, word, live) for zc, word in groups]

    def attend(panel, groups):
        raw = jnp.dot(panel, targets_t[...], preferred_element_type=jnp.float32)
        wide = panel.astype(jnp.float32)
        norms = lax.rsqrt(jnp.sum(wide * wide, axis=1, keepdims=True) + 1e-06)
        weights = jnp.exp2(raw * norms * target_scale - shift)
        flags = []
        for zc, there_y, there_x, word, live in groups:
            block = (zc * NY + there_y) * NX + there_x
            wanted = first_bits if word == 0 else bits
            if live is not None:
                wanted = jnp.where(live, wanted, 0)
            row = rep * (STRIDE // 8) + word
            mine = own_e[block, pl.ds(row, 1), :] & wanted
            other = sib_e[block, pl.ds(row, 1), :] & wanted
            flags.append(jnp.concatenate([mine, other], axis=1))
        weights = jnp.where(jnp.concatenate(flags, axis=0) != 0, weights, 0.0)
        total[...] += jnp.sum(weights.reshape(-1, 8, 2 * ROWS), axis=0)
        acc[...] += lax.dot_general(
            weights.astype(jnp.bfloat16), panel, (((0,), (0,)), ((), ())), preferred_element_type=jnp.float32
        )

    def z_landing(slot, frm):
        zc = lax.rem(frm + NZ, NZ)
        rows_in = column.at[pl.ds(pl.multiple_of(zc * PART, 16), PART)]
        return remote(rows_in, rows_in, z_send.at[slot], z_recv.at[slot], sibling)

    own_copy.wait()
    z_landing(0, zl - 1).wait_recv()
    z_landing(1, zl + 1).wait_recv()
    z_landing(2, zl + 2).wait_recv()

    col_a = column.at[pl.ds(0, UA)]
    col_b = column.at[pl.ds(UA, UB)]

    def ax_copy(slot, to, src=None):
        return remote(col_a, ax.at[slot], ax_send.at[slot], ax_recv.at[slot], to)

    def ay_copy(src, k, side):
        to = (y_up, y_down)[side]
        return remote(src, ay.at[k, side], ay_send.at[k, side], ay_recv.at[k, side], to)

    def by_copy(src, p, side, slot):
        to = (y_up, y_down)[side]
        return remote(src, by.at[p, slot], by_send.at[p, slot], by_recv.at[p, slot], to)

    def bx_copy(src, k, side):
        to = (x_up, x_down)[side]
        return remote(src, bx.at[k, side], bx_send.at[k, side], bx_recv.at[k, side], to)

    by_copy(col_b, 0, 0, 0).start()
    by_copy(col_b, 0, 1, 1).start()
    ax_copy(0, x_up).start()
    ax_copy(1, x_down).start()
    ax_copy(2, x_far).start()
    bx_copy(col_b, 0, 0).start()
    bx_copy(col_b, 0, 1).start()
    ay_copy(col_a, 0, 0).start()
    ay_copy(col_a, 0, 1).start()

    edge_load.wait()
    e_copy.wait_recv()
    attend(column[...], column_groups(A_GROUPS + B_GROUPS, 0, 0))

    for slot in range(3):
        ax_copy(slot, sibling).wait_recv()
        ay_copy(ax.at[slot], slot + 1, 0).start()
        ay_copy(ax.at[slot], slot + 1, 1).start()
    x_of = (-1, 1, 2)
    attend(
        ax[...].reshape(3 * UA, F),
        sum([column_groups(A_GROUPS, x_of[slot], 0) for slot in range(3)], []),
    )

    def step(k, carry):
        @pl.when(k < 4)
        def _():
            by_copy(col_b, k, 0, 0).wait_recv()

            @pl.when(k < 3)
            def _():
                by_copy(col_b, k, 1, 1).wait_recv()

            @pl.when(k < 2)
            def _():
                by_copy(by.at[k, 0], k + 1, 0, 0).start()
                by_copy(by.at[k, 1], k + 1, 1, 1).start()

            @pl.when(jnp.logical_and(k == 2, core == 0))
            def _():
                by_copy(by.at[2, 0], 3, 0, 0).start()

            @pl.when(jnp.logical_and(k == 2, core == 1))
            def _():
                by_copy(by.at[2, 1], 3, 1, 0).start()

            bx_copy(by.at[k, 0], 2 * k + 1, 0).start()
            bx_copy(by.at[k, 0], 2 * k + 1, 1).start()

            @pl.when(k < 3)
            def _():
                bx_copy(by.at[k, 1], 2 * k + 2, 0).start()
                bx_copy(by.at[k, 1], 2 * k + 2, 1).start()

            attend(
                by[k].reshape(2 * UB, F),
                column_groups(B_GROUPS, 0, -(k + 1)) + column_groups(B_GROUPS, 0, k + 1, k < 3),
            )

        ay_copy(col_a, k, 0).wait_recv()
        ay_copy(col_a, k, 1).wait_recv()

        @pl.when(k < 8)
        def _():
            ay_copy(ay.at[k, 0], k + 4, 0).start()
            ay_copy(ay.at[k, 1], k + 4, 1).start()

        @pl.when(jnp.logical_or(k == 8, k == 10))
        def _():
            ay_copy(ay.at[k, 0], 12 + lax.div(k - 8, 2), 0).start()

        @pl.when(jnp.logical_or(k == 9, k == 11))
        def _():
            ay_copy(ay.at[k, 1], 12 + lax.div(k - 8, 2), 1).start()

        far = k >= 12
        j0 = jnp.where(far, 2 * (k - 12), lax.rem(k, 4))
        j1 = jnp.where(far, 2 * (k - 12) + 1, lax.rem(k, 4))
        d = jnp.where(far, 4, 1 + lax.div(k, 4))

        def x_offset(j):
            return jnp.where(j == 0, 0, jnp.where(j == 1, -1, j - 1))

        attend(
            ay[k].reshape(2 * UA, F),
            column_groups(A_GROUPS, x_offset(j0), -d) + column_groups(A_GROUPS, x_offset(j1), d),
        )

        @pl.when(k < 12)
        def _():
            bx_copy(col_b, k, 0).wait_recv()
            bx_copy(col_b, k, 1).wait_recv()

            @pl.when(jnp.logical_and(k < 8, lax.rem(k, 2) == 0))
            def _():
                bx_copy(bx.at[k, 0], 8 + lax.div(k, 2), 0).start()

            @pl.when(jnp.logical_and(k < 8, lax.rem(k, 2) == 1))
            def _():
                bx_copy(bx.at[k, 1], 8 + lax.div(k, 2), 1).start()

            near = k < 8
            i0 = jnp.where(near, k, 2 * (k - 8))
            i1 = jnp.where(near, k, 2 * (k - 8) + 1)

            def y_offset(i):
                half = lax.div(i + 1, 2)
                return jnp.where(lax.rem(i, 2) == 1, -half, half)

            attend(
                bx[k].reshape(2 * UB, F),
                column_groups(B_GROUPS, jnp.where(near, -1, 2), y_offset(i0))
                + column_groups(B_GROUPS, jnp.where(near, 1, 2), y_offset(i1)),
            )

        return carry

    lax.fori_loop(0, 14, step, 0)

    tot = jnp.sum(total[...], axis=0, keepdims=True)
    tot_out[...] = jnp.broadcast_to(tot[:, ROWS:], (8, ROWS))
    fold = [
        remote(acc.at[pl.ds(ROWS, ROWS)], part_in, r_send.at[0], r_recv.at[0], sibling),
        remote(tot_out, tot_in, r_send.at[1], r_recv.at[1], sibling),
    ]
    for copy in fold:
        copy.start()
    for copy in fold:
        copy.wait_recv()
    red[rep] = (acc[pl.ds(0, ROWS)] + part_in[...]).astype(jnp.bfloat16)
    red_tot[rep] = tot[:, :ROWS] + tot_in[...]

    def share(slot, frm, to):
        return [
            remote(red.at[frm], red.at[frm], r_send.at[slot], r_recv.at[slot], to),
            remote(red_tot.at[frm], red_tot.at[frm], r_send.at[slot + 1], r_recv.at[slot + 1], to),
        ]

    shares = share(2, rep, r_up) + share(4, rep, r_down)
    for copy in shares:
        copy.start()
    for copy in share(2, lax.rem(rep + REPS - 1, REPS), r_up) + share(4, lax.rem(rep + 1, REPS), r_down):
        copy.wait_recv()
    sums = red[0].astype(jnp.float32) + red[1].astype(jnp.float32) + red[2].astype(jnp.float32)
    tots = red_tot[0] + red_tot[1] + red_tot[2]
    tall = jnp.broadcast_to(tots[0:1], (ROWS, ROWS)).T
    out[:, :ROWS] = (sums[:, :ROWS] / tall).astype(jnp.bfloat16)
    out[:, ROWS:] = (sums[:, ROWS:] / tall).astype(jnp.bfloat16)

    for copy in z_copies + [p_copy, e_copy] + fold + shares:
        copy.wait_send()
    for slot in range(3):
        ax_copy(slot, sibling).wait_send()

    def drain(k, carry):
        ay_copy(col_a, k, 0).wait_send()
        ay_copy(col_a, k, 1).wait_send()

        @pl.when(k < 12)
        def _():
            bx_copy(col_b, k, 0).wait_send()
            bx_copy(col_b, k, 1).wait_send()

        @pl.when(k < 4)
        def _():
            by_copy(col_b, k, 0, 0).wait_send()

        @pl.when(k < 3)
        def _():
            by_copy(col_b, k, 1, 1).wait_send()

        return carry

    lax.fori_loop(0, 14, drain, 0)


def on_device(features, weight, beta, edge_bits):
    edges = edge_bits.reshape(NX * NY * NZ, 2, 16, ROWS)
    anywhere = pl.BlockSpec(memory_space=pl.ANY)
    bf16, f32, i32 = jnp.bfloat16, jnp.float32, jnp.int32
    dma = pltpu.SemaphoreType.DMA
    return pl.pallas_call(
        kernel,
        out_shape=jax.ShapeDtypeStruct((ROWS, F), bf16),
        in_specs=[anywhere, anywhere, pl.BlockSpec(memory_space=pltpu.SMEM), anywhere],
        out_specs=pl.BlockSpec(memory_space=pltpu.VMEM),
        scratch_shapes=[
            pltpu.VMEM((ROWS, F), bf16),
            pltpu.VMEM((F, F), bf16),
            pltpu.VMEM((ROWS, F), bf16),
            pltpu.VMEM((ROWS, F), bf16),
            pltpu.VMEM((REPS, PART, F), bf16),
            pltpu.VMEM((F, 2 * ROWS), bf16),
            pltpu.VMEM((NX * NY * NZ, 16, ROWS), i32),
            pltpu.VMEM((NX * NY * NZ, 16, ROWS), i32),
            pltpu.VMEM((COLUMN, F), bf16),
            pltpu.VMEM((3, UA, F), bf16),
            pltpu.VMEM((14, 2, UA, F), bf16),
            pltpu.VMEM((4, 2, UB, F), bf16),
            pltpu.VMEM((12, 2, UB, F), bf16),
            pltpu.VMEM((2 * ROWS, F), f32),
            pltpu.VMEM((8, 2 * ROWS), f32),
            pltpu.VMEM((ROWS, F), f32),
            pltpu.VMEM((8, ROWS), f32),
            pltpu.VMEM((8, ROWS), f32),
            pltpu.VMEM((REPS, ROWS, F), bf16),
            pltpu.VMEM((REPS, 8, ROWS), f32),
            dma((2,)), dma, dma((3,)), dma((3,)), dma((2,)), dma((2,)),
            dma((3,)), dma((3,)), dma((14, 2)), dma((14, 2)), dma((4, 2)), dma((4, 2)), dma((12, 2)), dma((12, 2)),
            dma((6,)), dma((6,)),
        ],
        compiler_params=pltpu.CompilerParams(collective_id=0, has_side_effects=True),
    )(features, weight, beta, edges)


def solution(mesh):
    return jax.shard_map(
        on_device,
        mesh=mesh,
        in_specs=(P("rows", None), P(), P(), P(None, None, "rows")),
        out_specs=P("rows", None),
        check_vma=False,
    )
```

time: 1230 us -> 66.1 us (0.05)
  waiting for transfers between devices: 846 us -> 0 us
  starting transfers between devices: 170 us -> 0 us
  matrix products: 90.3 us -> 0 us
  other arithmetic: 72.4 us -> 0 us
  Pallas kernels: 0 us -> 63.8 us
  between operations: 14.1 us -> 0.66 us
    ppermute x87 -> x0, waiting for transfers between devices: 775 us -> none  [shifted(): lax.ppermute(shard, axis, [(i, (i + by) % length) for i in range(length)])]
    ppermute x87 -> x0, starting transfers between devices: 170 us -> none  [shifted(): lax.ppermute(shard, axis, [(i, (i + by) % length) for i in range(length)])]
    dot_general x173 -> x0, matrix products: 90.3 us -> none  [the longest x86 72.3 us: tile_terms(): lax.dot_general(source_panel, target_rows, (((1,), (1,)), ((), ())), pref...]
    psum x1 -> x0, waiting for transfers between devices: 70.8 us -> none  [on_device(): totals, weighted = lax.psum((final[1], final[2]), 'rep')]
    pallas_call x0 -> x1, Pallas kernels: none -> 63.8 us  [on_device(): pl.pallas_call(kernel, out_shape=jax.ShapeDtypeStruct((ROWS, F), bf16), i...]
    select_n x86 -> x0, other arithmetic: 60.5 us -> none  [accumulate(): packed = jnp.where(section_no < block_count, packed, 0)]
  transfers between devices with their start and end apart: 88 -> 0, of which waited for: 88 -> 0; matrix products, arithmetic and copies ran while one was open for 6% -> 0% of each run, Pallas kernels for 0% -> 0%
where the time goes in v1:
time: 66.1 us; the launch traced here: 65.9 us
  Pallas kernels  63.8 us (97%)
  local copies, waits for them, and re-layouts  1.47 us (2%)
    pallas_call x1, Pallas kernels, on_device(): pl.pallas_call(kernel, out_shape=jax.ShapeDtypeStruct((ROWS, F), bf16), i...  63.8 us
    unnamed x1, local copies, waits for them, and re-layouts  1.47 us

profile of v1, /device:TPU:1, one launch (start us, length us, event | category | flops | bytes accessed | tf_op | source)
XLA Modules:
  0.0 65.9 jit_solution(6767120026167619536)
XLA Ops:
  0.7 63.8 %shard_map.46 = bf16[128,256]{1,0:T(8,128)(2,1)} custom-call(bf16[128,256]{1,0:T(8,128)(2,1)} %features.1, bf16[256,256]{1,0:T(8,128)(2,1)} %weight.1, f32[1]{0:T(128)S(6)} %copy.6.beta, s32[128,2,16,128]{3,2,1,0:T(8,128)} %bitcast.1), custom_call_target="tpu_custom_call" | custom-call | tf_op jit(solution)/shard_map/pallas_call | solution.py:345
  64.4 1.5 %copy.7 = bf16[128,256]{1,0:T(8,128)(2,1)} copy(bf16[128,256]{1,0:T(8,128)(2,1)} %shard_map.46) | data formatting | bytes 131072
